TPU v7x, 256 devices: a whole 4x4x8 slice. The times are simulated.
256 devices in a mesh: row: 8 (over x_lo, y), col: 32 (over z, x_hi, core).
Axes of the slice: x: 4 (x_hi: 2, x_lo: 2; x = x_hi * 2 + x_lo), y: 4, z: 8, core: 2. Of those that a mesh axis runs over, the one named last changes fastest.
Arguments:
- b_steps: float32 [2, 1024, 8192], P(None, 'row', 'col'), may hold values from -6 to 6
- b_trail: float32 [8192, 8192], P('row', 'col'), may hold values from -6 to 6
- l_cross: float32 [1024, 1024], P('row', 'col'), may hold values from -0.1875 to 0.1875
- l_trail: float32 [2, 8192, 1024], P(None, 'row', 'col'), may hold values from -0.125 to 0.125
- diag_inv: float32 [2, 2, 512, 512], P(None, None, None, 'col'), may hold values from -1.5 to 1.5, as said below
- diag_low: float32 [2, 512, 512], P(None, None, 'col'), may hold values from -0.25 to 0.25
Outputs:
- x_steps: float32 [2, 1024, 8192], P(None, 'row', 'col')
- trail_out: float32 [8192, 8192], P('row', 'col')
Inputs may be any that keep to these rules, and one draw needn't show every extreme that they name: Each diag_inv[s, h] is lower triangular with diagonal entries of 0.5 to 1.5 and strictly lower entries of magnitude at most 3 / sqrt(512).
All inputs are finite; a program needn't handle non-finite values.
Results may differ from a plain program's by a relative error of at most 0.00013.
Values sent between devices are 32-bit elements; how exact they have to be, the bound alone decides.
A program may use at most 64 MiB of HBM per device.

v0:
```python
import jax
import jax.numpy as jnp
from jax import lax
from jax.sharding import PartitionSpec as P

exact_prec = lax.Precision.HIGHEST


def mult(left_mat, right_mat):
    return jnp.dot(left_mat, right_mat, precision=exact_prec, preferred_element_type=jnp.float32)


def inverse_columns(diag_inv, diag_low, section, offset, own_rows):
    inv_first = diag_inv[section, 0]
    inv_second = diag_inv[section, 1]
    low_block = diag_low[section]
    second_all, low_all = (
        lax.all_gather(inv_second, "col", axis=1, tiled=True),
        lax.all_gather(low_block, "col", axis=1, tiled=True),
    )
    left_cols = jnp.concatenate([inv_first, -mult(second_all, mult(low_all, inv_first))], 0)
    right_cols = jnp.concatenate([jnp.zeros_like(inv_second), inv_second], 0)
    left_all, right_all = (
        lax.all_gather(left_cols, "col", axis=1, tiled=True),
        lax.all_gather(right_cols, "col", axis=1, tiled=True),
    )
    whole = jnp.concatenate([left_all, right_all], 1)
    return lax.dynamic_slice_in_dim(whole, offset, own_rows, 1)


def solve_step(diag_inv, diag_low, section, offset, own_rows, rows_block):
    inverse_cols = inverse_columns(diag_inv, diag_low, section, offset, own_rows)
    return lax.psum(mult(inverse_cols, rows_block), "row")


def shards(b_steps, b_trail, l_cross, l_trail, diag_inv, diag_low):
    own_rows = b_steps.shape[1]
    offset = lax.axis_index("row") * own_rows
    solved_first = solve_step(diag_inv, diag_low, 0, offset, own_rows, b_steps[0])
    segment = solved_first
    next_rows = b_steps[1] - mult(lax.all_gather(l_cross, "col", axis=1, tiled=True), segment)
    trail = b_trail - mult(lax.all_gather(l_trail[0], "col", axis=1, tiled=True), segment)
    solved_second = solve_step(diag_inv, diag_low, 1, offset, own_rows, next_rows)
    segment = solved_second
    trail = trail - mult(lax.all_gather(l_trail[1], "col", axis=1, tiled=True), segment)
    mine_first = lax.dynamic_slice_in_dim(solved_first, offset, own_rows, 0)
    mine_second = lax.dynamic_slice_in_dim(solved_second, offset, own_rows, 0)
    return (jnp.stack([mine_first, mine_second]), trail)


def solution(mesh):
    placed = (
        P(None, "row", "col"),
        P("row", "col"),
        P("row", "col"),
        P(None, "row", "col"),
        P(None, None, None, "col"),
        P(None, None, "col"),
    )
    return jax.shard_map(
        shards,
        mesh=mesh,
        in_specs=placed,
        out_specs=(P(None, "row", "col"), P("row", "col")),
        check_vma=False,
    )
```

profile of v0, /device:TPU:1, one launch (start us, length us, event | category | flops | bytes accessed | tf_op | source)
XLA Modules:
  0.0 1003.2 jit_solution(6268098617561068982)
XLA Ops:
  7.2 0.0 all-gather.25.cloned.1.call-start
  7.2 1.4 fusion.38
  8.6 0.0 all-gather.25.cloned.1.call-update
  8.6 0.0 all-gather.27.cloned.1.call-start
  8.7 1.4 slice_bitcast_fusion.4
  10.1 0.0 all-gather.27.cloned.1.call-update
  10.2 0.0 all-gather.19.cloned.1.call-start
  10.2 0.6 concatenate.19
  10.8 0.0 all-gather.19.cloned.1.call-update
  10.9 0.0 all-gather.17.cloned.1.call-start
  10.9 82.2 %all-gather.25.cloned.1.call-done = f32[1,512,512]{1,2,0:T(8,128)} async-done(((f32[1,512,16]{1,2,0:T(8,128)}), f32[1,512,512]{1,2,0:T(8,128)}) %all-gather.25.cloned.1.call-update) | async-done | bytes 1048592 | tf_op jit(solution)/shard_map/all_gather | solution.py:19
  93.1 3.0 fusion.23
  96.2 74.2 %all-gather.27.cloned.1.call-done = f32[1,1,512,512]{2,3,1,0:T(8,128)} async-done(((f32[1,1,512,16]{2,3,1,0:T(8,128)}), f32[1,1,512,512]{2,3,1,0:T(8,128)}) %all-gather.27.cloned.1.call-update) | async-done | bytes 1048592 | tf_op jit(solution)/shard_map/all_gather | solution.py:18
  170.4 1.8 fusion.18
  172.2 0.6 pad_maximum_fusion.1
  172.8 0.0 all-gather.17.cloned.1.call-update
  172.9 0.0 all-gather.29.cloned.1.call-start
  172.9 0.5 all-gather.29.cloned.1.call-update
  173.5 0.0 all-gather.31.cloned.1.call-start
  173.5 0.5 all-gather.31.cloned.1.call-update
  174.0 0.0 all-reduce.5.cloned.1.call-start
  174.1 0.0 copy-start.3
  174.1 0.0 copy-start.4
  174.1 0.0 copy-start.2
  174.1 76.5 %all-gather.19.cloned.1.call-done = f32[1024,512]{0,1:T(8,128)} async-done(((f32[1024,16]{0,1:T(8,128)}), f32[1024,512]{0,1:T(8,128)}) %all-gather.19.cloned.1.call-update) | async-done | bytes 2097168 | tf_op jit(solution)/shard_map/all_gather | solution.py:25
  250.6 79.8 %all-gather.17.cloned.1.call-done = f32[1024,512]{0,1:T(8,128)} async-done(((f32[1024,16]{0,1:T(8,128)}), f32[1024,512]{0,1:T(8,128)}) %all-gather.17.cloned.1.call-update) | async-done | bytes 2097168 | tf_op jit(solution)/shard_map/all_gather | solution.py:24
  330.4 3.1 fusion.29
  333.5 0.0 all-reduce.5.cloned.1.call-update
  333.5 0.0 all-gather.23.cloned.1.call-start
  333.5 0.6 concatenate.22
  334.2 0.1 all-gather.23.cloned.1.call-update
  334.2 0.0 all-gather.21.cloned.1.call-start
  334.3 72.9 %all-gather.29.cloned.1.call-done = f32[1,512,512]{1,2,0:T(8,128)} async-done(((f32[1,512,16]{1,2,0:T(8,128)}), f32[1,512,512]{1,2,0:T(8,128)}) %all-gather.29.cloned.1.call-update) | async-done | bytes 1048592 | tf_op jit(solution)/shard_map/all_gather | solution.py:19
  407.2 3.0 fusion.20
  410.3 74.1 %all-gather.31.cloned.1.call-done = f32[1,1,512,512]{2,3,1,0:T(8,128)} async-done(((f32[1,1,512,16]{2,3,1,0:T(8,128)}), f32[1,1,512,512]{2,3,1,0:T(8,128)}) %all-gather.31.cloned.1.call-update) | async-done | bytes 1048592 | tf_op jit(solution)/shard_map/all_gather | solution.py:18
  484.3 1.8 fusion.17
  486.1 0.6 pad_maximum_fusion.2
  486.8 0.0 all-gather.21.cloned.1.call-update
  486.8 0.0 all-gather.35.cloned.1.call-start
  486.9 0.0 copy-done.3
  486.9 0.7 fusion.37
  487.6 0.0 all-gather.35.cloned.1.call-update
  487.6 0.0 all-reduce.7.cloned.1.call-start
  487.7 40.3 %all_gather.41 = f32[128,1024]{0,1:T(8,128)S(1)} all-gather(f32[128,32]{0,1:T(8,128)S(1)} %copy-done.4), channel_id=1, replica_groups=mesh['row'=8,'col'=32] {'col'}, dimensions={1}, use_global_device_ids=true | all-gather | bytes 540672 | tf_op jit(solution)/shard_map/all_gather | solution.py:41
  527.9 34.2 %all-reduce.5.cloned.1.call-done = f32[1024,256]{1,0:T(8,128)} async-done(((f32[1024,256]{1,0:T(8,128)}), f32[1024,256]{1,0:T(8,128)}) %all-reduce.5.cloned.1.call-update) | async-done | bytes 1048592 | tf_op jit(solution)/shard_map/psum | solution.py:33
  562.1 0.0 copy-done.2
  562.1 2.2 fusion.16
  564.4 0.0 copy-start
  564.4 85.6 %all-gather.23.cloned.1.call-done = f32[1024,512]{0,1:T(8,128)} async-done(((f32[1024,16]{0,1:T(8,128)}), f32[1024,512]{0,1:T(8,128)}) %all-gather.23.cloned.1.call-update) | async-done | bytes 2097168 | tf_op jit(solution)/shard_map/all_gather | solution.py:25
  649.9 79.4 %all-gather.21.cloned.1.call-done = f32[1024,512]{0,1:T(8,128)} async-done(((f32[1024,16]{0,1:T(8,128)}), f32[1024,512]{0,1:T(8,128)}) %all-gather.21.cloned.1.call-update) | async-done | bytes 2097168 | tf_op jit(solution)/shard_map/all_gather | solution.py:24
  729.3 3.0 fusion.26
  732.4 0.0 all-reduce.7.cloned.1.call-update
  732.4 0.2 all-gather.33.cloned.1.call-start
  732.6 0.3 all-gather.33.cloned.1.call-update
  733.0 0.3 copy.8
  733.3 0.0 copy-done
  733.3 82.1 %all-gather.35.cloned.1.call-done = f32[1,1024,1024]{1,2,0:T(8,128)} async-done(((f32[1,1024,32]{1,2,0:T(8,128)}), f32[1,1024,1024]{1,2,0:T(8,128)}) %all-gather.35.cloned.1.call-update) | async-done | bytes 4194320 | tf_op jit(solution)/shard_map/all_gather | solution.py:45
  815.4 76.7 %all-reduce.7.cloned.1.call-done = f32[1024,256]{1,0:T(8,128)} async-done(((f32[1024,256]{1,0:T(8,128)}), f32[1024,256]{1,0:T(8,128)}) %all-reduce.7.cloned.1.call-update) | async-done | bytes 1048592 | tf_op jit(solution)/shard_map/psum | solution.py:33
  892.2 7.1 fusion.13
  899.2 88.0 %all-gather.33.cloned.1.call-done = f32[1,1024,1024]{1,2,0:T(8,128)} async-done(((f32[1,1024,32]{1,2,0:T(8,128)}), f32[1,1024,1024]{1,2,0:T(8,128)}) %all-gather.33.cloned.1.call-update) | async-done | bytes 4194320 | tf_op jit(solution)/shard_map/all_gather | solution.py:42
  987.3 6.1 fusion.10
  993.4 1.3 copy.9
  994.7 0.9 dynamic-slice_bitcast_fusion
  995.6 0.7 pad_maximum_fusion
  (4 shorter events, 0.0 us)
Async XLA Ops:
  7.2 86.0 %all-gather.25.cloned.1.call-start = ((), (), s32[]{:S(2)}) async-start(), calls=%async_computation.6 | async-start | bytes 1081344 | tf_op jit(solution)/shard_map/all_gather | solution.py:19
  8.6 161.7 %all-gather.27.cloned.1.call-start = ((), (), s32[]{:S(2)}) async-start(), calls=%async_computation.7 | async-start | bytes 1081344 | tf_op jit(solution)/shard_map/all_gather | solution.py:18
  10.2 240.4 %all-gather.19.cloned.1.call-start = ((), (), s32[]{:S(2)}) async-start(), calls=%async_computation.1 | async-start | bytes 2162688 | tf_op jit(solution)/shard_map/all_gather | solution.py:25
  10.9 319.5 %all-gather.17.cloned.1.call-start = ((), (), s32[]{:S(2)}) async-start(), calls=%async_computation | async-start | bytes 2162688 | tf_op jit(solution)/shard_map/all_gather | solution.py:24
  172.9 234.4 %all-gather.29.cloned.1.call-start = ((), (), s32[]{:S(2)}) async-start(), calls=%async_computation.8 | async-start | bytes 1081344 | tf_op jit(solution)/shard_map/all_gather | solution.py:19
  173.5 310.9 %all-gather.31.cloned.1.call-start = ((), (), s32[]{:S(2)}) async-start(), calls=%async_computation.9 | async-start | bytes 1081344 | tf_op jit(solution)/shard_map/all_gather | solution.py:18
  174.0 388.1 %all-reduce.5.cloned.1.call-start = ((), (), s32[]{:S(2)}) async-start(), calls=%async_computation.2 | async-start | bytes 2097152 | tf_op jit(solution)/shard_map/psum | solution.py:33
  174.1 312.8 %copy-start.3 = (f32[2,1024,32]{1,2,0:T(8,128)S(1)}, f32[2,1024,32]{1,2,0:T(8,128)}, u32[]{:S(2)}) copy-start(f32[2,1024,32]{1,2,0:T(8,128)} %param.9) | copy-start | bytes 786436
  174.1 313.6 %copy-start.4 = (f32[128,32]{0,1:T(8,128)S(1)}, f32[128,32]{0,1:T(8,128)}, u32[]{:S(2)}) copy-start(f32[128,32]{0,1:T(8,128)} %param.8) | copy-start | bytes 49156
  174.1 388.0 %copy-start.2 = (f32[2,128,256]{2,1,0:T(8,128)S(1)}, f32[2,128,256]{2,1,0:T(8,128)}, u32[]{:S(2)}) copy-start(f32[2,128,256]{2,1,0:T(8,128)} %param.6) | copy-start | bytes 786436
  333.5 316.4 %all-gather.23.cloned.1.call-start = ((), (), s32[]{:S(2)}) async-start(), calls=%async_computation.4 | async-start | bytes 2162688 | tf_op jit(solution)/shard_map/all_gather | solution.py:25
  334.2 395.1 %all-gather.21.cloned.1.call-start = ((), (), s32[]{:S(2)}) async-start(), calls=%async_computation.3 | async-start | bytes 2162688 | tf_op jit(solution)/shard_map/all_gather | solution.py:24
  486.8 328.6 %all-gather.35.cloned.1.call-start = ((), (), s32[]{:S(2)}) async-start(), calls=%async_computation.11 | async-start | bytes 4325376 | tf_op jit(solution)/shard_map/all_gather | solution.py:45
  487.6 404.5 %all-reduce.7.cloned.1.call-start = ((), (), s32[]{:S(2)}) async-start(), calls=%async_computation.5 | async-start | bytes 2097152 | tf_op jit(solution)/shard_map/psum | solution.py:33
  527.9 205.0 %copy-start.1 = (f32[1024,256]{1,0:T(8,128)S(1)}, f32[1024,256]{1,0:T(8,128)}, u32[]{:S(2)}) copy-start(f32[1024,256]{1,0:T(8,128)} %param.7) | copy-start | bytes 3145732
  564.4 169.0 %copy-start = (f32[1024,256]{1,0:T(8,128)S(1)}, f32[1024,256]{1,0:T(8,128)}, u32[]{:S(2)}) copy-start(f32[1024,256]{1,0:T(8,128)} %all-reduce.5.cloned.1.call-done) | copy-start | bytes 3145732
  732.4 254.9 %all-gather.33.cloned.1.call-start = ((), (), s32[]{:S(2)}) async-start(), calls=%async_computation.10 | async-start | bytes 4325376 | tf_op jit(solution)/shard_map/all_gather | solution.py:42
Sparse Core Ops, SparseCore 0:
  11.4 81.7 all-gather.24
  95.9 74.3 all-gather.26
  173.7 76.8 all-gather.18
  253.8 76.5 all-gather.16
  333.0 74.1 all-gather.28
  409.9 74.3 all-gather.30
  487.5 74.5 all-reduce.4
  564.9 84.9 all-gather.22
  652.7 76.5 all-gather.20
  732.0 83.4 all-gather.34
  818.6 73.4 all-reduce.6
  895.4 91.8 all-gather.32
where the time goes:
time: 1000 us
  waiting for transfers between devices  907 us (91%)
  blocking collectives  40.3 us (4%)
  matrix products  31.2 us (3%)
  between operations  14.3 us (1%)
    all_gather x2, waiting for transfers between devices, inverse_columns(): lax.all_gather(right_cols, 'col', axis=1, tiled=True)  162 us
    all_gather x2, waiting for transfers between devices, inverse_columns(): lax.all_gather(left_cols, 'col', axis=1, tiled=True)  159 us
    all_gather x2, waiting for transfers between devices, inverse_columns(): lax.all_gather(low_block, 'col', axis=1, tiled=True)  155 us
    all_gather x2, waiting for transfers between devices, inverse_columns(): lax.all_gather(inv_second, 'col', axis=1, tiled=True)  148 us
    psum x2, waiting for transfers between devices, solve_step(): return lax.psum(mult(inverse_cols, rows_block), 'row')  111 us
    all_gather x1, waiting for transfers between devices, shards(): lax.all_gather(l_trail[0], 'col', axis=1, tiled=True)  88 us
    all_gather x1, waiting for transfers between devices, shards(): lax.all_gather(l_trail[1], 'col', axis=1, tiled=True)  82.1 us
    all_gather x1, blocking collectives, shards(): lax.all_gather(l_cross, 'col', axis=1, tiled=True)  40.3 us
  transfers between devices with their start and end apart: 12, of which 12 were waited for; matrix products, arithmetic and copies ran while one was open for 3% of the time, Pallas kernels for 0%

commit v1 on v0

--- a/solution.py
+++ b/solution.py
@@ -30,7 +30,7 @@
 
 def solve_step(diag_inv, diag_low, section, offset, own_rows, rows_block):
     inverse_cols = inverse_columns(diag_inv, diag_low, section, offset, own_rows)
-    return lax.psum(mult(inverse_cols, rows_block), "row")
+    return jnp.sum(lax.all_gather(mult(inverse_cols, rows_block), "row"), axis=0)
 
 
 def shards(b_steps, b_trail, l_cross, l_trail, diag_inv, diag_low):

time: 1000 us -> 1030 us (1.030)
  waiting for transfers between devices: 907 us -> 925 us
    all_gather x0 -> x2, waiting for transfers between devices: none -> 143 us  [solve_step(): lax.all_gather(mult(inverse_cols, rows_block), 'row')]
    psum x2 -> x0, waiting for transfers between devices: 111 us -> none  [solve_step(): return lax.psum(mult(inverse_cols, rows_block), 'row')]
where the time goes in v1:
time: 1030 us
  waiting for transfers between devices  925 us (90%)
  blocking collectives  40.7 us (4%)
  matrix products  29.7 us (3%)
  between operations  14.3 us (1%)
    all_gather x2, waiting for transfers between devices, inverse_columns(): lax.all_gather(left_cols, 'col', axis=1, tiled=True)  160 us
    all_gather x2, waiting for transfers between devices, inverse_columns(): lax.all_gather(low_block, 'col', axis=1, tiled=True)  155 us
    all_gather x2, waiting for transfers between devices, inverse_columns(): lax.all_gather(right_cols, 'col', axis=1, tiled=True)  153 us
    all_gather x2, waiting for transfers between devices, inverse_columns(): lax.all_gather(inv_second, 'col', axis=1, tiled=True)  148 us
    all_gather x2, waiting for transfers between devices, solve_step(): lax.all_gather(mult(inverse_cols, rows_block), 'row')  143 us
    all_gather x1, waiting for transfers between devices, shards(): lax.all_gather(l_trail[1], 'col', axis=1, tiled=True)  84.8 us
    all_gather x1, waiting for transfers between devices, shards(): lax.all_gather(l_trail[0], 'col', axis=1, tiled=True)  80 us
    all_gather x1, blocking collectives, shards(): lax.all_gather(l_cross, 'col', axis=1, tiled=True)  40.7 us
  transfers between devices with their start and end apart: 12, of which 12 were waited for; matrix products, arithmetic and copies ran while one was open for 3% of the time, Pallas kernels for 0%

profile of v1, /device:TPU:1, one launch (start us, length us, event | category | flops | bytes accessed | tf_op | source)
XLA Modules:
  0.0 1027.5 jit_solution(6968894013418319829)
XLA Ops:
  7.2 0.0 all-gather.29.cloned.1.call-start
  7.2 1.4 fusion.38
  8.6 0.0 all-gather.29.cloned.1.call-update
  8.6 0.0 all-gather.31.cloned.1.call-start
  8.7 1.4 slice_bitcast_fusion.4
  10.1 0.0 all-gather.31.cloned.1.call-update
  10.2 0.0 all-gather.23.cloned.1.call-start
  10.2 0.6 concatenate.19
  10.8 0.0 all-gather.23.cloned.1.call-update
  10.9 0.0 all-gather.21.cloned.1.call-start
  10.9 82.2 %all-gather.29.cloned.1.call-done = f32[1,512,512]{1,2,0:T(8,128)} async-done(((f32[1,512,16]{1,2,0:T(8,128)}), f32[1,512,512]{1,2,0:T(8,128)}) %all-gather.29.cloned.1.call-update) | async-done | bytes 1048592 | tf_op jit(solution)/shard_map/all_gather | solution.py:19
  93.1 3.0 fusion.23
  96.2 74.2 %all-gather.31.cloned.1.call-done = f32[1,1,512,512]{2,3,1,0:T(8,128)} async-done(((f32[1,1,512,16]{2,3,1,0:T(8,128)}), f32[1,1,512,512]{2,3,1,0:T(8,128)}) %all-gather.31.cloned.1.call-update) | async-done | bytes 1048592 | tf_op jit(solution)/shard_map/all_gather | solution.py:18
  170.4 1.8 fusion.18
  172.2 0.6 pad_maximum_fusion.1
  172.8 0.0 all-gather.21.cloned.1.call-update
  172.9 0.0 all-gather.35.cloned.1.call-start
  172.9 0.5 all-gather.35.cloned.1.call-update
  173.5 0.0 all-gather.37.cloned.1.call-start
  173.5 0.5 all-gather.37.cloned.1.call-update
  174.0 0.0 all-gather.33.cloned.1.call-start
  174.1 0.0 copy-start.3
  174.1 76.5 %all-gather.23.cloned.1.call-done = f32[1024,512]{0,1:T(8,128)} async-done(((f32[1024,16]{0,1:T(8,128)}), f32[1024,512]{0,1:T(8,128)}) %all-gather.23.cloned.1.call-update) | async-done | bytes 2097168 | tf_op jit(solution)/shard_map/all_gather | solution.py:25
  250.6 79.8 %all-gather.21.cloned.1.call-done = f32[1024,512]{0,1:T(8,128)} async-done(((f32[1024,16]{0,1:T(8,128)}), f32[1024,512]{0,1:T(8,128)}) %all-gather.21.cloned.1.call-update) | async-done | bytes 2097168 | tf_op jit(solution)/shard_map/all_gather | solution.py:24
  330.4 3.1 fusion.29
  333.5 0.0 all-gather.33.cloned.1.call-update
  333.5 0.0 all-gather.27.cloned.1.call-start
  333.5 0.6 concatenate.22
  334.2 0.1 all-gather.27.cloned.1.call-update
  334.2 0.0 all-gather.25.cloned.1.call-start
  334.3 72.9 %all-gather.35.cloned.1.call-done = f32[1,512,512]{1,2,0:T(8,128)} async-done(((f32[1,512,16]{1,2,0:T(8,128)}), f32[1,512,512]{1,2,0:T(8,128)}) %all-gather.35.cloned.1.call-update) | async-done | bytes 1048592 | tf_op jit(solution)/shard_map/all_gather | solution.py:19
  407.2 3.0 fusion.20
  410.3 74.1 %all-gather.37.cloned.1.call-done = f32[1,1,512,512]{2,3,1,0:T(8,128)} async-done(((f32[1,1,512,16]{2,3,1,0:T(8,128)}), f32[1,1,512,512]{2,3,1,0:T(8,128)}) %all-gather.37.cloned.1.call-update) | async-done | bytes 1048592 | tf_op jit(solution)/shard_map/all_gather | solution.py:18
  484.3 1.8 fusion.17
  486.1 0.6 pad_maximum_fusion.2
  486.8 0.0 all-gather.25.cloned.1.call-update
  486.8 0.0 all-gather.39.cloned.1.call-start
  486.9 0.0 copy-done.3
  486.9 40.7 %all_gather.55 = f32[128,1024]{0,1:T(8,128)S(1)} all-gather(f32[128,32]{0,1:T(8,128)S(1)} %copy-done.3), channel_id=1, replica_groups=mesh['row'=8,'col'=32] {'col'}, dimensions={1}, use_global_device_ids=true | all-gather | bytes 540672 | tf_op jit(solution)/shard_map/all_gather | solution.py:41
  527.5 54.2 %all-gather.33.cloned.1.call-done = f32[8192,256]{1,0:T(8,128)} async-done(((f32[1024,256]{1,0:T(8,128)}), f32[8192,256]{1,0:T(8,128)}) %all-gather.33.cloned.1.call-update) | async-done | bytes 8388624 | tf_op jit(solution)/shard_map/all_gather | solution.py:33
  581.8 4.1 reduce_sum.18
  585.9 0.0 copy-done.1
  585.9 0.0 copy-start.2
  585.9 1.0 fusion.16
  586.9 0.0 copy-start
  586.9 76.1 %all-gather.27.cloned.1.call-done = f32[1024,512]{0,1:T(8,128)} async-done(((f32[1024,16]{0,1:T(8,128)}), f32[1024,512]{0,1:T(8,128)}) %all-gather.27.cloned.1.call-update) | async-done | bytes 2097168 | tf_op jit(solution)/shard_map/all_gather | solution.py:25
  663.1 80.0 %all-gather.25.cloned.1.call-done = f32[1024,512]{0,1:T(8,128)} async-done(((f32[1024,16]{0,1:T(8,128)}), f32[1024,512]{0,1:T(8,128)}) %all-gather.25.cloned.1.call-update) | async-done | bytes 2097168 | tf_op jit(solution)/shard_map/all_gather | solution.py:24
  743.0 3.0 fusion.26
  746.1 0.0 all-gather.39.cloned.1.call-update
  746.1 0.0 all-gather.43.cloned.1.call-start
  746.2 0.0 copy-done.2
  746.2 0.7 fusion.37
  746.9 0.0 all-gather.43.cloned.1.call-update
  746.9 0.2 all-gather.41.cloned.1.call-start
  747.1 0.3 all-gather.41.cloned.1.call-update
  747.5 0.3 copy.8
  747.8 89.1 %all-gather.39.cloned.1.call-done = f32[8192,256]{1,0:T(8,128)} async-done(((f32[1024,256]{1,0:T(8,128)}), f32[8192,256]{1,0:T(8,128)}) %all-gather.39.cloned.1.call-update) | async-done | bytes 8388624 | tf_op jit(solution)/shard_map/all_gather | solution.py:33
  836.9 4.1 reduce_sum.19
  841.0 84.8 %all-gather.43.cloned.1.call-done = f32[1,1024,1024]{1,2,0:T(8,128)} async-done(((f32[1,1024,32]{1,2,0:T(8,128)}), f32[1,1024,1024]{1,2,0:T(8,128)}) %all-gather.43.cloned.1.call-update) | async-done | bytes 4194320 | tf_op jit(solution)/shard_map/all_gather | solution.py:45
  925.8 6.8 fusion.13
  932.5 80.0 %all-gather.41.cloned.1.call-done = f32[1,1024,1024]{1,2,0:T(8,128)} async-done(((f32[1,1024,32]{1,2,0:T(8,128)}), f32[1,1024,1024]{1,2,0:T(8,128)}) %all-gather.41.cloned.1.call-update) | async-done | bytes 4194320 | tf_op jit(solution)/shard_map/all_gather | solution.py:42
  1012.5 6.1 fusion.10
  1018.6 1.3 copy.9
  1019.9 0.7 pad_maximum_fusion
  (4 shorter events, 0.0 us)
Async XLA Ops:
  7.2 86.0 %all-gather.29.cloned.1.call-start = ((), (), s32[]{:S(2)}) async-start(), calls=%async_computation.4 | async-start | bytes 1081344 | tf_op jit(solution)/shard_map/all_gather | solution.py:19
  8.6 161.7 %all-gather.31.cloned.1.call-start = ((), (), s32[]{:S(2)}) async-start(), calls=%async_computation.5 | async-start | bytes 1081344 | tf_op jit(solution)/shard_map/all_gather | solution.py:18
  10.2 240.4 %all-gather.23.cloned.1.call-start = ((), (), s32[]{:S(2)}) async-start(), calls=%async_computation.1 | async-start | bytes 2162688 | tf_op jit(solution)/shard_map/all_gather | solution.py:25
  10.9 319.5 %all-gather.21.cloned.1.call-start = ((), (), s32[]{:S(2)}) async-start(), calls=%async_computation | async-start | bytes 2162688 | tf_op jit(solution)/shard_map/all_gather | solution.py:24
  172.9 234.4 %all-gather.35.cloned.1.call-start = ((), (), s32[]{:S(2)}) async-start(), calls=%async_computation.7 | async-start | bytes 1081344 | tf_op jit(solution)/shard_map/all_gather | solution.py:19
  173.5 310.9 %all-gather.37.cloned.1.call-start = ((), (), s32[]{:S(2)}) async-start(), calls=%async_computation.8 | async-start | bytes 1081344 | tf_op jit(solution)/shard_map/all_gather | solution.py:18
  174.0 407.7 %all-gather.33.cloned.1.call-start = ((), (), s32[]{:S(2)}) async-start(), calls=%async_computation.6 | async-start | bytes 9437184 | tf_op jit(solution)/shard_map/all_gather | solution.py:33
  174.1 312.8 %copy-start.3 = (f32[128,32]{0,1:T(8,128)S(1)}, f32[128,32]{0,1:T(8,128)}, u32[]{:S(2)}) copy-start(f32[128,32]{0,1:T(8,128)} %param.8) | copy-start | bytes 49156
  333.5 329.6 %all-gather.27.cloned.1.call-start = ((), (), s32[]{:S(2)}) async-start(), calls=%async_computation.3 | async-start | bytes 2162688 | tf_op jit(solution)/shard_map/all_gather | solution.py:25
  334.2 408.8 %all-gather.25.cloned.1.call-start = ((), (), s32[]{:S(2)}) async-start(), calls=%async_computation.2 | async-start | bytes 2162688 | tf_op jit(solution)/shard_map/all_gather | solution.py:24
  486.8 350.1 %all-gather.39.cloned.1.call-start = ((), (), s32[]{:S(2)}) async-start(), calls=%async_computation.9 | async-start | bytes 9437184 | tf_op jit(solution)/shard_map/all_gather | solution.py:33
  581.8 4.1 copy-start.1
  585.9 160.3 %copy-start.2 = (f32[2,1024,32]{1,2,0:T(8,128)S(1)}, f32[2,1024,32]{1,2,0:T(8,128)}, u32[]{:S(2)}) copy-start(f32[2,1024,32]{1,2,0:T(8,128)} %param.9) | copy-start | bytes 786436
  586.9 160.6 %copy-start = (f32[1024,256]{1,0:T(8,128)S(1)}, f32[1024,256]{1,0:T(8,128)}, u32[]{:S(2)}) copy-start(f32[1024,256]{1,0:T(8,128)} %param.7) | copy-start | bytes 3145732
  746.1 179.7 %all-gather.43.cloned.1.call-start = ((), (), s32[]{:S(2)}) async-start(), calls=%async_computation.11 | async-start | bytes 4325376 | tf_op jit(solution)/shard_map/all_gather | solution.py:45
  746.9 265.6 %all-gather.41.cloned.1.call-start = ((), (), s32[]{:S(2)}) async-start(), calls=%async_computation.10 | async-start | bytes 4325376 | tf_op jit(solution)/shard_map/all_gather | solution.py:42
Sparse Core Ops, SparseCore 0:
  11.4 81.7 all-gather.28
  95.9 74.3 all-gather.30
  173.7 76.8 all-gather.22
  253.8 76.5 all-gather.20
  333.0 74.1 all-gather.34
  409.9 74.3 all-gather.36
  486.7 95.0 all-gather.32
  584.5 78.4 all-gather.26
  666.4 76.5 all-gather.24
  746.2 90.6 all-gather.38
  839.7 86.0 all-gather.42
  929.0 83.4 all-gather.40
